TPU v7x, 32 devices: a whole 2x2x4 slice. The times are simulated.
32 devices in a mesh: groups: 2 (over y), seq: 4 (over z), head: 2 (over x), sub: 2 (over core).
Axes of the slice: x: 2, y: 2, z: 4, core: 2. Of those that a mesh axis runs over, the one named last changes fastest.
Arguments:
- wave_pieces: float32 [8, 2, 2, 64, 3072], P(('groups', 'seq'), 'head', 'sub'), parts along dimension 0, may hold values from -6 to 6
- piece_target: int32 [8, 2, 2, 64], P(('groups', 'seq'), 'head', 'sub'), parts along dimension 0, may hold values from -1 to 127, as said below
- utt_lengths: int32 [8], P('groups'), parts along dimension 0, may hold values from 1 to 1088, 2176 in all
- sub_weight: bfloat16 [512, 1536], P(None, 'head'), may hold values from -2 to 2
- sub_bias: bfloat16 [1536], P('head'), may hold values from -4 to 4
- norm_gain: float32 [1536], replicated, may hold values from 0.1 to 1.9
- qkv_weight: bfloat16 [1536, 3, 1536], P(None, None, 'head'), may hold values from -0.21875 to 0.21875
- rel_bias: float32 [24, 543], P('head'), may hold values from -4 to 250
Outputs:
- context: bfloat16 [4352, 1536], P(('groups', 'seq', 'sub'), 'head'), parts along dimension 0
There are 2 independent parts, one for each index of `groups`. A program takes and returns all parts, laid end to end along the dimension named above; an argument that names none is the same for every part. Nothing has to cross between parts.
Inputs may be any that keep to these rules, and one draw needn't show every extreme that they name: `piece_target`: each value is -1 (an empty slot) or s * 32 + p, naming piece p of seq index s for the loader's own head and sub indices. Every piece of every eighth is named by exactly one slot of a loader with the same head and sub indices. A loader names at most 16 pieces of one seq index; in every draw some loaders name exactly 16 pieces of every seq index, so that all their slots are full.
All inputs are finite; a program needn't handle non-finite values.
Results may differ from a plain program's by a relative error of at most 0.006.
Values may be sent and summed in bfloat16 or wider, within the bound.
A program may use at most 64 MiB of HBM per device.

v0:
```python
import functools
import math

import jax
import jax.numpy as jnp
import numpy as np
from jax import lax
from jax.experimental import pallas as pl
from jax.experimental.pallas import tpu as pltpu
from jax.sharding import PartitionSpec as P

HDIM = 64
MEL = 128
NFFT = 512
HOP = 160
FP = 17
CH = 136
PE = 32
LANES = 128
TABLE = 640


SAMPLE_RATE = 16000.0
EPSILON = 1e-05
MASKED = -1e30
MESH = pl.DeviceIdType.MESH


def split_bf16(table):
    high = table.astype(np.float32).astype(jnp.bfloat16)
    low = (table - high.astype(np.float64)).astype(np.float32).astype(jnp.bfloat16)
    return np.stack([high, low])


def window_table():
    return (0.5 - 0.5 * np.cos(2.0 * np.pi / NFFT * np.arange(NFFT)))[None].astype(np.float32)


def fourier_tables():
    half = NFFT // 2
    sample = np.arange(half)[:, None]

    def phase(bins):
        return (sample * bins[None, :] % NFFT) * (2.0 * np.pi / NFFT)

    even, odd = np.arange(0, half, 2), np.arange(1, half, 2)
    even_sine = np.sin(phase(even))
    even_sine[:, 0] = np.cos(phase(np.array([half])))[:, 0]
    even_table = np.concatenate([np.cos(phase(even)), even_sine], axis=1)
    odd_table = np.concatenate([np.cos(phase(odd)), np.sin(phase(odd))], axis=1)
    return np.stack([split_bf16(even_table), split_bf16(odd_table)])


def mel_table():
    bin_total = NFFT // 2 + 1
    highest = 2595.0 * math.log10(1.0 + SAMPLE_RATE / 2.0 / 700.0)
    points = np.arange(MEL + 2) * (highest / (MEL + 1))
    hertz = 700.0 * (np.power(10.0, points / 2595.0) - 1.0)
    centres = np.arange(bin_total) * (SAMPLE_RATE / NFFT)
    rising = (centres[:, None] - hertz[None, :-2]) / (hertz[1:-1] - hertz[:-2])[None, :]
    falling = (hertz[None, 2:] - centres[:, None]) / (hertz[2:] - hertz[1:-1])[None, :]
    table = np.maximum(0.0, np.minimum(rising, falling))
    sine_even = table[0 : bin_total - 1 : 2].copy()
    sine_even[0] = table[bin_total - 1]
    rows = np.concatenate(
        [table[0 : bin_total - 1 : 2], sine_even, table[1::2], table[1::2]], axis=0
    )
    return split_bf16(rows)


def dot(left, right):
    return jnp.dot(left, right, preferred_element_type=jnp.float32)


def dot_split(value, high, low):
    value_high = value.astype(jnp.bfloat16)
    value_low = (value - value_high.astype(jnp.float32)).astype(jnp.bfloat16)
    return dot(value_high, high) + dot(value_low, high) + dot(value_high, low)


def front_kernel(
    shards, heads, subs,
    wave_ref, target_ref, weight_ref, window_ref, fourier_ref, mel_ref,
    tokens_ref, weights_ref,
    mel_rows, packed, received,
    wsend, wrecv, fsend, frecv, asend, arecv, hsend, hrecv, nsend, nrecv,
):
    s, h, u = lax.axis_index("seq"), lax.axis_index("head"), lax.axis_index("sub")
    half = s * subs + u
    halves = shards * subs
    slots = wave_ref.shape[0]
    cap = slots // shards
    depth = weight_ref.shape[0] // subs

    def place_of(index):
        return {"seq": index // subs, "sub": index % subs}

    barrier = pltpu.get_barrier_semaphore()
    for d in range(1, shards):
        pl.semaphore_signal(
            barrier, inc=1, device_id={"seq": lax.rem(s + d, shards)}, device_id_type=MESH
        )
    for d in range(1, heads):
        pl.semaphore_signal(
            barrier, inc=1, device_id={"head": lax.rem(h + d, heads)}, device_id_type=MESH
        )

    @pl.when(half > 0)
    def _():
        for other in range(heads):
            pl.semaphore_signal(
                barrier, inc=1, device_id={**place_of(half - 1), "head": other},
                device_id_type=MESH,
            )

    @pl.when(half < halves - 1)
    def _():
        for other in range(heads):
            pl.semaphore_signal(
                barrier, inc=1, device_id={**place_of(half + 1), "head": other},
                device_id_type=MESH,
            )

    inner = jnp.where(half > 0, heads, 0) + jnp.where(half < halves - 1, heads, 0)
    pl.semaphore_wait(barrier, shards - 1 + heads - 1 + inner)

    weight_copies = []
    for d in range(1, heads):
        copy = pltpu.make_async_remote_copy(
            src_ref=weight_ref.at[pl.ds(u * depth, depth)],
            dst_ref=weights_ref.at[h, pl.ds(u * depth, depth)],
            send_sem=wsend.at[d - 1],
            recv_sem=wrecv.at[d - 1],
            device_id={"head": lax.rem(h + d, heads)},
            device_id_type=MESH,
        )
        copy.start()
        weight_copies.append(copy)

    for shift in range(4):
        wave = wave_ref[...]
        if shift:
            wave = pltpu.roll(wave, wave.shape[1] - 32 * shift, 1)
        groups = range((FP - shift + 3) // 4)
        frames = [
            wave[:, LANES * (5 * g + shift) : LANES * (5 * g + shift) + NFFT] * window_ref[...]
            for g in groups
        ]
        frames = jnp.concatenate(frames, axis=0)
        low, high = frames[:, : NFFT // 2], frames[:, NFFT // 2 :]
        even = dot_split(low + high, fourier_ref[0, 0], fourier_ref[0, 1])
        odd = dot_split(low - high, fourier_ref[1, 0], fourier_ref[1, 1])
        squares = jnp.concatenate([even * even, odd * odd], axis=1)
        energy = dot_split(squares, mel_ref[0], mel_ref[1])
        logs = jnp.log(1.0 + energy).astype(jnp.bfloat16)
        for g in groups:
            f = 4 * g + shift
            mel_rows[:, f * MEL : (f + 1) * MEL] = logs[g * slots : (g + 1) * slots]

    target = target_ref[...]
    owner = jnp.where(target >= 0, lax.shift_right_arithmetic(target, 5), shards)
    place = jnp.bitwise_and(target, PE - 1)
    down = lax.broadcasted_iota(jnp.int32, (slots, slots), 0)
    across = lax.broadcasted_iota(jnp.int32, (slots, slots), 1)
    owner_wide = jnp.broadcast_to(owner, (slots, slots))
    owner_down = jnp.sum(jnp.where(down == across, owner_wide, 0), axis=1, keepdims=True)
    rank = jnp.sum(
        jnp.where((owner_down == owner_wide) & (down < across), 1, 0), axis=0, keepdims=True
    )
    goal = jnp.where(owner < shards, owner * cap + rank, -1)
    chosen = down == goal
    select = chosen.astype(jnp.float32).astype(jnp.bfloat16)
    rows = dot(select, mel_rows[...]).astype(jnp.bfloat16)
    code = jnp.sum(jnp.where(chosen, place + 1, 0), axis=1, keepdims=True).astype(jnp.float32)
    code = jnp.broadcast_to(code, (slots, LANES)).astype(jnp.bfloat16)
    for t in range(shards):
        packed[t, :, : FP * MEL] = rows[t * cap : (t + 1) * cap]
        packed[t, :, FP * MEL :] = code[t * cap : (t + 1) * cap]

    piece_copies = []
    for d in range(1, shards):
        to = lax.rem(s + d, shards)
        copy = pltpu.make_async_remote_copy(
            src_ref=packed.at[to],
            dst_ref=received.at[s],
            send_sem=asend.at[d - 1],
            recv_sem=arecv.at[d - 1],
            device_id={"seq": to},
            device_id_type=MESH,
        )
        copy.start()
        piece_copies.append(copy)
    received[s] = packed[s]
    weights_ref[h] = weight_ref[...]

    @pl.when(half == 0)
    def _():
        tokens_ref[0] = jnp.zeros(tokens_ref.shape[1:], tokens_ref.dtype)

    @pl.when(half == halves - 1)
    def _():
        tokens_ref[heads + 1] = jnp.zeros(tokens_ref.shape[1:], tokens_ref.dtype)

    for copy in piece_copies:
        copy.wait_recv()

    arrived = received[...]
    if cap % 16:
        arrived = arrived.astype(jnp.float32).reshape(slots, arrived.shape[2])
        arrived = arrived.astype(jnp.bfloat16)
    else:
        arrived = arrived.reshape(slots, arrived.shape[2])
    frame_rows = jnp.concatenate(
        [arrived[:, f * MEL : (f + 1) * MEL] for f in range(FP)], axis=0
    )
    code_down = arrived[:, FP * MEL : FP * MEL + 1].astype(jnp.float32)
    code_wide = jnp.broadcast_to(code_down, (slots, slots))
    code_across = jnp.sum(jnp.where(down == across, code_wide, 0.0), axis=0, keepdims=True)
    first = jnp.where(code_across > 0.5, (code_across - 1.0) * FP, -1000.0)
    frame_at = jnp.concatenate([first + float(f) for f in range(FP)], axis=1)
    for m in range(4):
        token = lax.broadcasted_iota(jnp.int32, (CH, FP * slots), 0) * 4 + m
        pick = (token.astype(jnp.float32) == frame_at).astype(jnp.float32).astype(jnp.bfloat16)
        tokens_ref[h + 1, :, m * MEL : (m + 1) * MEL] = dot(pick, frame_rows).astype(jnp.bfloat16)

    head_copies = []
    for d in range(1, heads):
        copy = pltpu.make_async_remote_copy(
            src_ref=tokens_ref.at[h + 1],
            dst_ref=tokens_ref.at[h + 1],
            send_sem=hsend.at[d - 1],
            recv_sem=hrecv.at[d - 1],
            device_id={"head": lax.rem(h + d, heads)},
            device_id_type=MESH,
        )
        copy.start()
        head_copies.append(copy)

    def halo(other, to, row, side):
        return pltpu.make_async_remote_copy(
            src_ref=tokens_ref.at[h + 1],
            dst_ref=tokens_ref.at[row],
            send_sem=nsend.at[side, other],
            recv_sem=nrecv.at[side],
            device_id={**place_of(to), "head": other},
            device_id_type=MESH,
        )

    sends_up = (half < halves - 1) & (h == heads - 1)
    sends_down = (half > 0) & (h == 0)

    @pl.when(sends_up)
    def _():
        for other in range(heads):
            halo(other, half + 1, 0, 0).start()

    @pl.when(sends_down)
    def _():
        for other in range(heads):
            halo(other, half - 1, heads + 1, 1).start()

    sibling = {"sub": lax.rem(u + 1, subs)}
    forward_copies = []
    for d in range(1, heads):
        weight_copies[d - 1].wait_recv()
        source = lax.rem(h - d + heads, heads)
        copy = pltpu.make_async_remote_copy(
            src_ref=weights_ref.at[source, pl.ds(u * depth, depth)],
            dst_ref=weights_ref.at[source, pl.ds(u * depth, depth)],
            send_sem=fsend.at[d - 1],
            recv_sem=frecv.at[d - 1],
            device_id=sibling,
            device_id_type=MESH,
        )
        copy.start()
        forward_copies.append(copy)

    for copy in head_copies:
        copy.wait_recv()

    @pl.when(half > 0)
    def _():
        halo(0, half, 0, 0).wait_recv()

    @pl.when(half < halves - 1)
    def _():
        halo(0, half, heads + 1, 1).wait_recv()

    for copy in forward_copies:
        copy.wait_recv()
    for copy in weight_copies + piece_copies + head_copies + forward_copies:
        copy.wait_send()

    @pl.when(sends_up)
    def _():
        for other in range(heads):
            halo(other, half + 1, 0, 0).wait_send()

    @pl.when(sends_down)
    def _():
        for other in range(heads):
            halo(other, half - 1, heads + 1, 1).wait_send()


def back_kernel(
    tokens_ref, weights_ref, sub_bias_ref, gain_ref, qkv_ref, table_ref, lengths_ref, first_ref,
    context_ref,
    qkv_weight, queries, keys, values, bias, sem,
):
    blocks = tokens_ref.shape[0] - 2
    heads = weights_ref.shape[0]
    width = weights_ref.shape[2]
    loads = [
        pltpu.make_async_copy(qkv_ref.at[part], qkv_weight.at[part], sem.at[part])
        for part in range(3)
    ]
    for load in loads:
        load.start()
    first_token, token_total = first_ref[0], first_ref[1]

    normed = []
    for b in range(blocks + 2):
        summed = jnp.concatenate(
            [dot(tokens_ref[b], weights_ref[g]) for g in range(heads)], axis=1
        )
        summed = summed + sub_bias_ref[...].astype(jnp.float32)
        value = (summed / (1.0 + jnp.exp(-summed))).astype(jnp.bfloat16).astype(jnp.float32)
        mean = jnp.mean(value, axis=1, keepdims=True)
        centred = value - mean
        variance = jnp.mean(centred * centred, axis=1, keepdims=True)
        normed.append(
            (centred * lax.rsqrt(variance + EPSILON) * gain_ref[...]).astype(jnp.bfloat16)
        )

    for part, out in ((0, queries), (1, keys), (2, values)):
        loads[part].wait()
        for b in range(blocks + 2):
            if part == 0 and (b == 0 or b == blocks + 1):
                continue
            row = (b - 1 if part == 0 else b) * CH
            done = dot(normed[b], qkv_weight[part]).astype(jnp.bfloat16).astype(jnp.float32)
            if part == 0:
                done = done * (1.0 / math.sqrt(HDIM))
            out[row : row + CH] = done

    span = 3 * CH
    masks = []
    for b in range(blocks):
        query_pos = first_token + b * CH + lax.broadcasted_iota(jnp.int32, (CH, 1), 0)
        key_pos = first_token + (b - 1) * CH + lax.broadcasted_iota(jnp.int32, (1, span), 1)
        end = jnp.int32(0)
        query_utt = jnp.zeros_like(query_pos)
        key_utt = jnp.zeros_like(key_pos)
        for r in range(lengths_ref.shape[0]):
            end = end + lengths_ref[r]
            query_utt = query_utt + (query_pos >= end).astype(jnp.int32)
            key_utt = key_utt + (key_pos >= end).astype(jnp.int32)
        inside = (key_pos >= 0) & (key_pos < token_total)
        key_utt = jnp.where(inside, key_utt, -1)
        masks.append(query_utt == key_utt)

    lane = lax.broadcasted_iota(jnp.int32, (1, LANES), 1)
    for pair in range(width // LANES):
        lanes = slice(pair * LANES, (pair + 1) * LANES)
        for e in range(2):
            row = jnp.broadcast_to(table_ref[2 * pair + e : 2 * pair + e + 1, :], (CH, TABLE))
            rolled = pltpu.roll(row, TABLE - (CH - 1), 1, stride=1, stride_axis=0)
            bias[e] = rolled[:, :span]
        for b in range(blocks):
            query = queries[b * CH : (b + 1) * CH, lanes]
            key = keys[b * CH : b * CH + span, lanes].astype(jnp.bfloat16)
            value = values[b * CH : b * CH + span, lanes].astype(jnp.bfloat16)
            outs = []
            for e in range(2):
                mine = (lane < HDIM) if e == 0 else (lane >= HDIM)
                own = jnp.where(mine, query, 0.0).astype(jnp.bfloat16)
                scores = lax.dot_general(
                    own, key, (((1,), (1,)), ((), ())), preferred_element_type=jnp.float32
                )
                scores = jnp.where(masks[b], scores + bias[e], MASKED)
                raised = jnp.exp(scores - jnp.max(scores, axis=1, keepdims=True))
                share = 1.0 / jnp.sum(raised, axis=1, keepdims=True)
                outs.append(dot((raised * share).astype(jnp.bfloat16), value))
            joined = jnp.where(lane < HDIM, outs[0], outs[1]).astype(jnp.bfloat16)
            context_ref[b * CH : (b + 1) * CH, lanes] = joined


def local(
    shards, heads, subs,
    wave_pieces, piece_target, utt_lengths, sub_weight, sub_bias, norm_gain, qkv_weight, rel_bias,
):
    slots, samples = wave_pieces.shape[3:]
    cap = slots // shards
    depth, width = sub_weight.shape
    whole_width = qkv_weight.shape[0]
    vmem = pl.BlockSpec(memory_space=pltpu.VMEM)
    smem = pl.BlockSpec(memory_space=pltpu.SMEM)
    payload = (FP + 1) * MEL
    dma = pltpu.SemaphoreType.DMA
    tokens, weights = pl.pallas_call(
        functools.partial(front_kernel, shards, heads, subs),
        out_shape=(
            jax.ShapeDtypeStruct((heads + 2, CH, 4 * MEL), jnp.bfloat16),
            jax.ShapeDtypeStruct((heads, depth, width), jnp.bfloat16),
        ),
        in_specs=[vmem] * 6,
        out_specs=(vmem, vmem),
        scratch_shapes=[
            pltpu.VMEM((slots, FP * MEL), jnp.bfloat16),
            pltpu.VMEM((shards, cap, payload), jnp.bfloat16),
            pltpu.VMEM((shards, cap, payload), jnp.bfloat16),
            dma((heads - 1,)), dma((heads - 1,)), dma((heads - 1,)), dma((heads - 1,)),
            dma((shards - 1,)), dma((shards - 1,)),
            dma((heads - 1,)), dma((heads - 1,)),
            dma((2, heads)), dma((2,)),
        ],
        compiler_params=pltpu.CompilerParams(
            collective_id=0, has_side_effects=True, vmem_limit_bytes=48 << 20
        ),
        name="front",
    )(
        wave_pieces.reshape(slots, samples),
        piece_target.reshape(1, slots),
        sub_weight,
        jnp.asarray(window_table()),
        jnp.asarray(fourier_tables()),
        jnp.asarray(mel_table()),
    )

    tokens_here = heads * CH
    half = lax.axis_index("seq") * subs + lax.axis_index("sub")
    first = jnp.stack([half * tokens_here, jnp.int32(shards * subs * tokens_here)])
    bias_all = lax.all_gather(sub_bias, "head", axis=0, tiled=True)
    table = jnp.pad(rel_bias[:, ::-1], ((0, 0), (0, TABLE - rel_bias.shape[1])))
    return pl.pallas_call(
        back_kernel,
        out_shape=jax.ShapeDtypeStruct((tokens_here, width), jnp.bfloat16),
        in_specs=[vmem, vmem, vmem, vmem, pl.BlockSpec(memory_space=pl.ANY), vmem, smem, smem],
        out_specs=vmem,
        scratch_shapes=[
            pltpu.VMEM((3, whole_width, width), jnp.bfloat16),
            pltpu.VMEM((tokens_here, width), jnp.float32),
            pltpu.VMEM((tokens_here + 2 * CH, width), jnp.float32),
            pltpu.VMEM((tokens_here + 2 * CH, width), jnp.float32),
            pltpu.VMEM((2, CH, 3 * CH), jnp.float32),
            dma((3,)),
        ],
        compiler_params=pltpu.CompilerParams(vmem_limit_bytes=48 << 20),
        name="back",
    )(
        tokens,
        weights,
        bias_all.reshape(1, whole_width),
        norm_gain.reshape(1, whole_width),
        jnp.transpose(qkv_weight, (1, 0, 2)),
        table,
        utt_lengths,
        first,
    )


def solution(mesh):
    placed = (
        P(("groups", "seq"), "head", "sub", None, None),
        P(("groups", "seq"), "head", "sub", None),
        P("groups"),
        P(None, "head"),
        P("head"),
        P(),
        P(None, None, "head"),
        P("head", None),
    )
    return jax.shard_map(
        functools.partial(local, mesh.shape["seq"], mesh.shape["head"], mesh.shape["sub"]),
        mesh=mesh,
        in_specs=placed,
        out_specs=P(("groups", "seq", "sub"), "head"),
        check_vma=False,
    )
```

profile of v0, /device:TPU:1, one launch (start us, length us, event | category | flops | bytes accessed | tf_op | source)
XLA Modules:
  0.0 53.5 jit_solution(17354048927609970199)
XLA Ops:
  0.0 0.1 pad_add_fusion.first_ref
  0.1 0.7 %reshape.16 = bf16[1,1,768]{2,1,0:T(2,128)(2,1)S(1)} reshape(bf16[768]{0:T(1024)(128)(2,1)} %param.15) | data formatting | bytes 3072
  0.8 3.7 %all-gather = bf16[2,1,768]{2,1,0:T(2,128)(2,1)S(1)} all-gather(bf16[1,1,768]{2,1,0:T(2,128)(2,1)S(1)} %reshape.16), channel_id=1, replica_groups=mesh['groups'=2,'seq'=4,'head'=2,'sub'=2] {'head'}, dimensions={0}, use_global_device_ids=true | all-gather | bytes 4608 | tf_op jit(solution)/shard_map/all_gather | solution.py:433
  4.5 0.7 %reshape.15.gain_ref = f32[1,1536]{1,0:T(1,128)S(1)} reshape(f32[1536]{0:T(1024)} %param.16) | data formatting | bytes 12288 | tf_op jit(solution)/shard_map/reshape | solution.py:454
  5.2 2.3 %reverse = f32[12,640]{1,0:T(8,128)S(1)} reverse(f32[12,640]{1,0:T(8,128)} %bitcast.10), dimensions={1} | reverse | bytes 61440
  7.5 0.1 slice
  7.6 0.0 copy-start
  7.6 1.1 %copy-done = f32[1,1,1,64,3072]{4,3,2,1,0:T(8,128)S(1)} copy-done((f32[1,1,1,64,3072]{4,3,2,1,0:T(8,128)S(1)}, f32[1,1,1,64,3072]{4,3,2,1,0:T(8,128)}, u32[]{:S(2)}) %copy-start) | copy-done | bytes 786456
  8.7 0.0 copy-start.1
  8.7 1.1 %copy-done.1 = bf16[512,768]{1,0:T(8,128)(2,1)S(1)} copy-done((bf16[512,768]{1,0:T(8,128)(2,1)S(1)}, bf16[512,768]{1,0:T(8,128)(2,1)}, u32[]{:S(2)}) %copy-start.1) | copy-done | bytes 786456
  9.9 0.0 copy-start.2
  9.9 1.0 %copy-done.2 = bf16[2,2,256,256]{3,2,1,0:T(8,128)(2,1)S(1)} copy-done((bf16[2,2,256,256]{3,2,1,0:T(8,128)(2,1)S(1)}, bf16[2,2,256,256]{3,2,1,0:T(8,128)(2,1)}, u32[]{:S(2)}) %copy-start.2) | copy-done | bytes 524312
  10.9 0.0 copy-start.3
  10.9 0.9 %copy-done.3 = bf16[2,512,128]{2,1,0:T(8,128)(2,1)S(1)} copy-done((bf16[2,512,128]{2,1,0:T(8,128)(2,1)S(1)}, bf16[2,512,128]{2,1,0:T(8,128)(2,1)}, u32[]{:S(2)}) %copy-start.3) | copy-done | bytes 262168
  11.8 0.0 copy-start.4
  11.8 0.7 %copy-done.4 = f32[1,512]{1,0:T(1,128)S(1)} copy-done((f32[1,512]{1,0:T(1,128)S(1)}, f32[1,512]{1,0:T(1,128)}, u32[]{:S(2)}) %copy-start.4) | copy-done | bytes 2072
  12.5 0.0 copy-start.5
  12.5 0.7 %copy-done.5 = s32[1,1,1,64]{3,2,1,0:T(1,128)S(1)} copy-done((s32[1,1,1,64]{3,2,1,0:T(1,128)S(1)}, s32[1,1,1,64]{3,2,1,0:T(1,128)}, u32[]{:S(2)}) %copy-start.5) | copy-done | bytes 280
  13.2 22.1 %front.1 = (bf16[4,136,512]{2,1,0:T(8,128)(2,1)S(1)}, bf16[2,512,768]{2,1,0:T(8,128)(2,1)S(1)}) custom-call(f32[64,3072]{1,0:T(8,128)S(1)} %bitcast.6, s32[1,64]{1,0:T(1,128)S(1)} %bitcast.8, bf16[512,768]{1,0:T(8,128)(2,1)S(1)} %copy-done.1, f32[1,512]{1,0:T(1,128)S(1)} %copy-done.4, bf16[2,2,256,256]{3,2,1,0:T(8,128)(2,1)S(1)} %copy-done.2, ...), custom_call_target="tpu_custom_call" | custom-call | tf_op jit(solution)/shard_map/front/pallas_call | solution.py:400
  35.3 0.0 copy-start.6
  35.3 0.6 %copy-done.6 = s32[4]{0:T(128)S(1)} copy-done((s32[4]{0:T(128)S(1)}, s32[4]{0:T(128)}, u32[]{:S(2)}) %copy-start.6) | copy-done | bytes 40
  35.9 17.4 %back.1 = bf16[272,768]{1,0:T(8,128)(2,1)} custom-call(bf16[4,136,512]{2,1,0:T(8,128)(2,1)S(1)} %get-tuple-element.7.tokens_ref, bf16[2,512,768]{2,1,0:T(8,128)(2,1)S(1)} %get-tuple-element.8.weights_ref, bf16[1,1536]{1,0:T(2,128)(2,1)S(1)} %bitcast.7, f32[1,1536]{1,0:T(1,128)S(1)} %reshape.15.gain_ref, bf16[3,1536,768]{2,1,0:T(8,128)(2,1)} %bitcast.9, ...), custom_call_target="tpu_custom_call" | custom-call | tf_op jit(solution)/shard_map/back/pallas_call | solution.py:435
  (1 shorter events, 0.0 us)
Async XLA Ops:
  7.6 1.1 %copy-start = (f32[1,1,1,64,3072]{4,3,2,1,0:T(8,128)S(1)}, f32[1,1,1,64,3072]{4,3,2,1,0:T(8,128)}, u32[]{:S(2)}) copy-start(f32[1,1,1,64,3072]{4,3,2,1,0:T(8,128)} %param.11) | copy-start | bytes 2359300
  8.7 1.1 %copy-start.1 = (bf16[512,768]{1,0:T(8,128)(2,1)S(1)}, bf16[512,768]{1,0:T(8,128)(2,1)}, u32[]{:S(2)}) copy-start(bf16[512,768]{1,0:T(8,128)(2,1)} %weight_ref.1) | copy-start | bytes 2359300
  9.9 1.0 %copy-start.2 = (bf16[2,2,256,256]{3,2,1,0:T(8,128)(2,1)S(1)}, bf16[2,2,256,256]{3,2,1,0:T(8,128)(2,1)}, u32[]{:S(2)}) copy-start(bf16[2,2,256,256]{3,2,1,0:T(8,128)(2,1)} %constant.25.clone.fourier_ref) | copy-start | bytes 1572868
  10.9 0.9 %copy-start.3 = (bf16[2,512,128]{2,1,0:T(8,128)(2,1)S(1)}, bf16[2,512,128]{2,1,0:T(8,128)(2,1)}, u32[]{:S(2)}) copy-start(bf16[2,512,128]{2,1,0:T(8,128)(2,1)} %constant.26.clone.mel_ref) | copy-start | bytes 786436
  11.8 0.7 %copy-start.4 = (f32[1,512]{1,0:T(1,128)S(1)}, f32[1,512]{1,0:T(1,128)}, u32[]{:S(2)}) copy-start(f32[1,512]{1,0:T(1,128)} %constant.24.clone.window_ref) | copy-start | bytes 6148
  12.5 0.7 %copy-start.5 = (s32[1,1,1,64]{3,2,1,0:T(1,128)S(1)}, s32[1,1,1,64]{3,2,1,0:T(1,128)}, u32[]{:S(2)}) copy-start(s32[1,1,1,64]{3,2,1,0:T(1,128)} %param.12) | copy-start | bytes 772
  35.3 0.7 %copy-start.6 = (s32[4]{0:T(128)S(1)}, s32[4]{0:T(128)}, u32[]{:S(2)}) copy-start(s32[4]{0:T(128)} %lengths_ref.1) | copy-start | bytes 52
where the time goes:
time: 54.3 us; the launch traced here: 53.5 us
  Pallas kernels  39.5 us (73%)
  local copies, waits for them, and re-layouts  10 us (18%)
  blocking collectives  3.73 us (7%)
    pallas_call x1, Pallas kernels, local(): pl.pallas_call(functools.partial(front_kernel, shards, heads, subs), out_...  22.1 us
    pallas_call x1, Pallas kernels, local(): pl.pallas_call(back_kernel, out_shape=jax.ShapeDtypeStruct((tokens_here,...  17.4 us
    unnamed x17, local copies, waits for them, and re-layouts  9.3 us
    all_gather x1, blocking collectives, local(): bias_all = lax.all_gather(sub_bias, 'head', axis=0, tiled=True)  3.73 us

commit v1 on v0

--- a/solution.py
+++ b/solution.py
@@ -80,10 +80,11 @@
 
 def front_kernel(
     shards, heads, subs,
-    wave_ref, target_ref, weight_ref, window_ref, fourier_ref, mel_ref,
-    tokens_ref, weights_ref,
+    wave_in, target_in, weight_ref, window_in, fourier_in, mel_in, sub_bias_in, gain_in, rel_in,
+    tokens_ref, weights_ref, sub_bias_ref, gain_ref, bias_ref,
+    wave_ref, target_ref, window_ref, fourier_ref, mel_ref, sub_bias_row, gain_row, rel_ref,
     mel_rows, packed, received,
-    wsend, wrecv, fsend, frecv, asend, arecv, hsend, hrecv, nsend, nrecv,
+    lsem, wsend, wrecv, fsend, frecv, asend, arecv, hsend, hrecv, nsend, nrecv, bsend, brecv,
 ):
     s, h, u = lax.axis_index("seq"), lax.axis_index("head"), lax.axis_index("sub")
     half = s * subs + u
@@ -95,6 +96,15 @@
     def place_of(index):
         return {"seq": index // subs, "sub": index % subs}
 
+    pairs = (
+        (wave_in, wave_ref), (window_in, window_ref), (fourier_in, fourier_ref),
+        (mel_in, mel_ref), (target_in, target_ref), (sub_bias_in, sub_bias_row),
+        (gain_in, gain_row), (rel_in, rel_ref), (weight_ref, weights_ref.at[h]),
+    )
+    loads = [pltpu.make_async_copy(a, b, lsem.at[i]) for i, (a, b) in enumerate(pairs)]
+    for load in loads:
+        load.start()
+
     barrier = pltpu.get_barrier_semaphore()
     for d in range(1, shards):
         pl.semaphore_signal(
@@ -124,7 +134,7 @@
     inner = jnp.where(half > 0, heads, 0) + jnp.where(half < halves - 1, heads, 0)
     pl.semaphore_wait(barrier, shards - 1 + heads - 1 + inner)
 
-    weight_copies = []
+    weight_copies, bias_copies = [], []
     for d in range(1, heads):
         copy = pltpu.make_async_remote_copy(
             src_ref=weight_ref.at[pl.ds(u * depth, depth)],
@@ -137,6 +147,22 @@
         copy.start()
         weight_copies.append(copy)
 
+    loads[5].wait()
+    sub_bias_ref[h] = sub_bias_row[...].astype(jnp.float32).reshape(1, sub_bias_row.shape[0])
+    for d in range(1, heads):
+        copy = pltpu.make_async_remote_copy(
+            src_ref=sub_bias_ref.at[h],
+            dst_ref=sub_bias_ref.at[h],
+            send_sem=bsend.at[d - 1],
+            recv_sem=brecv.at[d - 1],
+            device_id={"head": lax.rem(h + d, heads)},
+            device_id_type=MESH,
+        )
+        copy.start()
+        bias_copies.append(copy)
+
+    for index in range(4):
+        loads[index].wait()
     for shift in range(4):
         wave = wave_ref[...]
         if shift:
@@ -157,6 +183,7 @@
             f = 4 * g + shift
             mel_rows[:, f * MEL : (f + 1) * MEL] = logs[g * slots : (g + 1) * slots]
 
+    loads[4].wait()
     target = target_ref[...]
     owner = jnp.where(target >= 0, lax.shift_right_arithmetic(target, 5), shards)
     place = jnp.bitwise_and(target, PE - 1)
@@ -191,7 +218,6 @@
         copy.start()
         piece_copies.append(copy)
     received[s] = packed[s]
-    weights_ref[h] = weight_ref[...]
 
     @pl.when(half == 0)
     def _():
@@ -200,6 +226,26 @@
     @pl.when(half == halves - 1)
     def _():
         tokens_ref[heads + 1] = jnp.zeros(tokens_ref.shape[1:], tokens_ref.dtype)
+
+    loads[6].wait()
+    gain_ref[...] = gain_row[...].reshape(gain_ref.shape)
+    loads[7].wait()
+    taps = rel_ref.shape[1]
+    mirror = lax.broadcasted_iota(jnp.int32, (taps, TABLE), 0) + lax.broadcasted_iota(
+        jnp.int32, (taps, TABLE), 1
+    )
+    mirror = (mirror == taps - 1).astype(jnp.float32).astype(jnp.bfloat16)
+    rest = rel_ref[...]
+    terms = []
+    for _ in range(3):
+        term = rest.astype(jnp.bfloat16)
+        rest = rest - term.astype(jnp.float32)
+        terms.append(dot(term, mirror))
+    flipped = terms[0] + (terms[1] + terms[2])
+    for row in range(rel_ref.shape[0]):
+        wide = jnp.broadcast_to(flipped[row : row + 1, :], (CH, TABLE))
+        rolled = pltpu.roll(wide, TABLE - (CH - 1), 1, stride=1, stride_axis=0)
+        bias_ref[row] = rolled[:, : 3 * CH]
 
     for copy in piece_copies:
         copy.wait_recv()
@@ -286,9 +332,10 @@
     def _():
         halo(0, half, heads + 1, 1).wait_recv()
 
-    for copy in forward_copies:
+    for copy in forward_copies + bias_copies:
         copy.wait_recv()
-    for copy in weight_copies + piece_copies + head_copies + forward_copies:
+    loads[8].wait()
+    for copy in bias_copies + weight_copies + piece_copies + head_copies + forward_copies:
         copy.wait_send()
 
     @pl.when(sends_up)
@@ -303,9 +350,10 @@
 
 
 def back_kernel(
-    tokens_ref, weights_ref, sub_bias_ref, gain_ref, qkv_ref, table_ref, lengths_ref, first_ref,
+    shards, subs,
+    tokens_ref, weights_ref, sub_bias_ref, gain_ref, bias_ref, qkv_ref, lengths_in,
     context_ref,
-    qkv_weight, queries, keys, values, bias, sem,
+    qkv_weight, queries, keys, values, lengths_ref, sem,
 ):
     blocks = tokens_ref.shape[0] - 2
     heads = weights_ref.shape[0]
@@ -314,16 +362,17 @@
         pltpu.make_async_copy(qkv_ref.at[part], qkv_weight.at[part], sem.at[part])
         for part in range(3)
     ]
+    loads.append(pltpu.make_async_copy(lengths_in, lengths_ref, sem.at[3]))
     for load in loads:
         load.start()
-    first_token, token_total = first_ref[0], first_ref[1]
+    half = lax.axis_index("seq") * subs + lax.axis_index("sub")
+    first_token, token_total = half * blocks * CH, shards * subs * blocks * CH
 
     normed = []
     for b in range(blocks + 2):
         summed = jnp.concatenate(
-            [dot(tokens_ref[b], weights_ref[g]) for g in range(heads)], axis=1
-        )
-        summed = summed + sub_bias_ref[...].astype(jnp.float32)
+            [dot(tokens_ref[b], weights_ref[g]) + sub_bias_ref[g] for g in range(heads)], axis=1
+        )
         value = (summed / (1.0 + jnp.exp(-summed))).astype(jnp.bfloat16).astype(jnp.float32)
         mean = jnp.mean(value, axis=1, keepdims=True)
         centred = value - mean
@@ -343,6 +392,7 @@
                 done = done * (1.0 / math.sqrt(HDIM))
             out[row : row + CH] = done
 
+    loads[3].wait()
     span = 3 * CH
     masks = []
     for b in range(blocks):
@@ -362,10 +412,6 @@
     lane = lax.broadcasted_iota(jnp.int32, (1, LANES), 1)
     for pair in range(width // LANES):
         lanes = slice(pair * LANES, (pair + 1) * LANES)
-        for e in range(2):
-            row = jnp.broadcast_to(table_ref[2 * pair + e : 2 * pair + e + 1, :], (CH, TABLE))
-            rolled = pltpu.roll(row, TABLE - (CH - 1), 1, stride=1, stride_axis=0)
-            bias[e] = rolled[:, :span]
         for b in range(blocks):
             query = queries[b * CH : (b + 1) * CH, lanes]
             key = keys[b * CH : b * CH + span, lanes].astype(jnp.bfloat16)
@@ -377,7 +423,7 @@
                 scores = lax.dot_general(
                     own, key, (((1,), (1,)), ((), ())), preferred_element_type=jnp.float32
                 )
-                scores = jnp.where(masks[b], scores + bias[e], MASKED)
+                scores = jnp.where(masks[b], scores + bias_ref[2 * pair + e], MASKED)
                 raised = jnp.exp(scores - jnp.max(scores, axis=1, keepdims=True))
                 share = 1.0 / jnp.sum(raised, axis=1, keepdims=True)
                 outs.append(dot((raised * share).astype(jnp.bfloat16), value))
@@ -394,68 +440,84 @@
     depth, width = sub_weight.shape
     whole_width = qkv_weight.shape[0]
     vmem = pl.BlockSpec(memory_space=pltpu.VMEM)
-    smem = pl.BlockSpec(memory_space=pltpu.SMEM)
     payload = (FP + 1) * MEL
     dma = pltpu.SemaphoreType.DMA
-    tokens, weights = pl.pallas_call(
+    hbm = pl.BlockSpec(memory_space=pltpu.HBM)
+    heads_here = rel_bias.shape[0]
+    tokens, weights, bias_rows, gain_row, position_bias = pl.pallas_call(
         functools.partial(front_kernel, shards, heads, subs),
         out_shape=(
             jax.ShapeDtypeStruct((heads + 2, CH, 4 * MEL), jnp.bfloat16),
             jax.ShapeDtypeStruct((heads, depth, width), jnp.bfloat16),
+            jax.ShapeDtypeStruct((heads, 1, width), jnp.float32),
+            jax.ShapeDtypeStruct((1, whole_width), jnp.float32),
+            jax.ShapeDtypeStruct((heads_here, CH, 3 * CH), jnp.float32),
         ),
-        in_specs=[vmem] * 6,
-        out_specs=(vmem, vmem),
+        in_specs=[hbm] * 9,
+        out_specs=(vmem,) * 5,
         scratch_shapes=[
+            pltpu.VMEM((slots, samples), jnp.float32),
+            pltpu.VMEM((1, slots), jnp.int32),
+            pltpu.VMEM((1, NFFT), jnp.float32),
+            pltpu.VMEM((2, 2, NFFT // 2, NFFT // 2), jnp.bfloat16),
+            pltpu.VMEM((2, NFFT, MEL), jnp.bfloat16),
+            pltpu.VMEM((width,), jnp.bfloat16),
+            pltpu.VMEM((whole_width,), jnp.float32),
+            pltpu.VMEM(rel_bias.shape, jnp.float32),
             pltpu.VMEM((slots, FP * MEL), jnp.bfloat16),
             pltpu.VMEM((shards, cap, payload), jnp.bfloat16),
             pltpu.VMEM((shards, cap, payload), jnp.bfloat16),
+            dma((9,)),
             dma((heads - 1,)), dma((heads - 1,)), dma((heads - 1,)), dma((heads - 1,)),
             dma((shards - 1,)), dma((shards - 1,)),
             dma((heads - 1,)), dma((heads - 1,)),
-            dma((2, heads)), dma((2,)),
+            dma((2, heads)), dma((2,)), dma((heads - 1,)), dma((heads - 1,)),
         ],
         compiler_params=pltpu.CompilerParams(
-            collective_id=0, has_side_effects=True, vmem_limit_bytes=48 << 20
+            collective_id=0, has_side_effects=True, vmem_limit_bytes=28 << 20
         ),
         name="front",
     )(
-        wave_pieces.reshape(slots, samples),
-        piece_target.reshape(1, slots),
-        sub_weight,
-        jnp.asarray(window_table()),
-        jnp.asarray(fourier_tables()),
-        jnp.asarray(mel_table()),
+        *[
+            pltpu.with_memory_space_constraint(value, pltpu.HBM)
+            for value in (
+                wave_pieces.reshape(slots, samples),
+                piece_target.reshape(1, slots),
+                sub_weight,
+                jnp.asarray(window_table()),
+                jnp.asarray(fourier_tables()),
+                jnp.asarray(mel_table()),
+                sub_bias,
+                norm_gain,
+                rel_bias,
+            )
+        ]
     )
 
     tokens_here = heads * CH
-    half = lax.axis_index("seq") * subs + lax.axis_index("sub")
-    first = jnp.stack([half * tokens_here, jnp.int32(shards * subs * tokens_here)])
-    bias_all = lax.all_gather(sub_bias, "head", axis=0, tiled=True)
-    table = jnp.pad(rel_bias[:, ::-1], ((0, 0), (0, TABLE - rel_bias.shape[1])))
     return pl.pallas_call(
-        back_kernel,
+        functools.partial(back_kernel, shards, subs),
         out_shape=jax.ShapeDtypeStruct((tokens_here, width), jnp.bfloat16),
-        in_specs=[vmem, vmem, vmem, vmem, pl.BlockSpec(memory_space=pl.ANY), vmem, smem, smem],
+        in_specs=[vmem] * 5 + [hbm, hbm],
         out_specs=vmem,
         scratch_shapes=[
             pltpu.VMEM((3, whole_width, width), jnp.bfloat16),
             pltpu.VMEM((tokens_here, width), jnp.float32),
             pltpu.VMEM((tokens_here + 2 * CH, width), jnp.float32),
             pltpu.VMEM((tokens_here + 2 * CH, width), jnp.float32),
-            pltpu.VMEM((2, CH, 3 * CH), jnp.float32),
-            dma((3,)),
+            pltpu.SMEM(utt_lengths.shape, jnp.int32),
+            dma((4,)),
         ],
-        compiler_params=pltpu.CompilerParams(vmem_limit_bytes=48 << 20),
+        compiler_params=pltpu.CompilerParams(vmem_limit_bytes=36 << 20),
         name="back",
     )(
         tokens,
         weights,
-        bias_all.reshape(1, whole_width),
-        norm_gain.reshape(1, whole_width),
-        jnp.transpose(qkv_weight, (1, 0, 2)),
-        table,
-        utt_lengths,
-        first,
+        bias_rows,
+        gain_row,
+        position_bias,
+        pltpu.with_memory_space_constraint(jnp.transpose(qkv_weight, (1, 0, 2)), pltpu.HBM),
+        pltpu.with_memory_space_constraint(utt_lengths, pltpu.HBM),
     )
 
 

time: 54.3 us -> 39.4 us (0.73)
  local copies, waits for them, and re-layouts: 10 us -> 0 us
  blocking collectives: 3.73 us -> 0 us
  Pallas kernels: 39.5 us -> 38.9 us
    unnamed x17 -> x0, local copies, waits for them, and re-layouts: 9.3 us -> none
    all_gather x1 -> x0, blocking collectives: 3.73 us -> none  [local(): bias_all = lax.all_gather(sub_bias, 'head', axis=0, tiled=True)]
    reshape x1 -> x0, local copies, waits for them, and re-layouts: 0.7 us -> none  [local(): norm_gain.reshape(1, whole_width)]
where the time goes in v1:
time: 39.4 us; the launch traced here: 39.1 us
  Pallas kernels  38.9 us (99%)
    pallas_call x1, Pallas kernels, local(): pl.pallas_call(functools.partial(front_kernel, shards, heads, subs), out_...  21.7 us
    pallas_call x1, Pallas kernels, local(): pl.pallas_call(functools.partial(back_kernel, shards, subs), out_shape=ja...  17.2 us

profile of v1, /device:TPU:1, one launch (start us, length us, event | category | flops | bytes accessed | tf_op | source)
XLA Modules:
  0.0 39.1 jit_solution(957881032880498556)
XLA Ops:
  0.0 21.7 %front.1 = (bf16[4,136,512]{2,1,0:T(8,128)(2,1)S(1)}, bf16[2,512,768]{2,1,0:T(8,128)(2,1)S(1)}, f32[2,1,768]{2,1,0:T(1,128)S(1)}, f32[1,1536]{1,0:T(1,128)S(1)}, f32[12,136,408]{2,1,0:T(8,128)S(1)}) custom-call(f32[64,3072]{1,0:T(8,128)} %bitcast.4, s32[1,64]{1,0:T(1,128)} %bitcast.5, bf16[512,768]{1,0:T(8,128)(2,1)} %weight_ref.1, ...), custom_call_target="tpu_custom_call" | custom-call | tf_op jit(solution)/shard_map/front/pallas_call | solution.py:447
  21.7 17.2 %back.1 = bf16[272,768]{1,0:T(8,128)(2,1)} custom-call(bf16[4,136,512]{2,1,0:T(8,128)(2,1)S(1)} %get-tuple-element.10.tokens_ref, bf16[2,512,768]{2,1,0:T(8,128)(2,1)S(1)} %get-tuple-element.11.weights_ref, f32[2,1,768]{2,1,0:T(1,128)S(1)} %get-tuple-element.12.sub_bias_ref, f32[1,1536]{1,0:T(1,128)S(1)} %get-tuple-element.13.gain_ref, ...), custom_call_target="tpu_custom_call" | custom-call | tf_op jit(solution)/shard_map/back/pallas_call | solution.py:498

commit v2 on v1

--- a/solution.py
+++ b/solution.py
@@ -83,7 +83,7 @@
     wave_in, target_in, weight_ref, window_in, fourier_in, mel_in, sub_bias_in, gain_in, rel_in,
     tokens_ref, weights_ref, sub_bias_ref, gain_ref, bias_ref,
     wave_ref, target_ref, window_ref, fourier_ref, mel_ref, sub_bias_row, gain_row, rel_ref,
-    mel_rows, packed, received,
+    packed_0, packed_1, packed_2, packed_3, received_0, received_1, received_2, received_3,
     lsem, wsend, wrecv, fsend, frecv, asend, arecv, hsend, hrecv, nsend, nrecv, bsend, brecv,
 ):
     s, h, u = lax.axis_index("seq"), lax.axis_index("head"), lax.axis_index("sub")
@@ -92,6 +92,9 @@
     slots = wave_ref.shape[0]
     cap = slots // shards
     depth = weight_ref.shape[0] // subs
+
+    packed = (packed_0, packed_1, packed_2, packed_3)
+    received = (received_0, received_1, received_2, received_3)
 
     def place_of(index):
         return {"seq": index // subs, "sub": index % subs}
@@ -161,6 +164,24 @@
         copy.start()
         bias_copies.append(copy)
 
+    loads[4].wait()
+    target = target_ref[...]
+    owner = jnp.where(target >= 0, lax.shift_right_arithmetic(target, 5), shards)
+    place = jnp.bitwise_and(target, PE - 1)
+    down = lax.broadcasted_iota(jnp.int32, (slots, slots), 0)
+    across = lax.broadcasted_iota(jnp.int32, (slots, slots), 1)
+    owner_wide = jnp.broadcast_to(owner, (slots, slots))
+    owner_down = jnp.sum(jnp.where(down == across, owner_wide, 0), axis=1, keepdims=True)
+    rank = jnp.sum(
+        jnp.where((owner_down == owner_wide) & (down < across), 1, 0), axis=0, keepdims=True
+    )
+    goal = jnp.where(owner < shards, owner * cap + rank, -1)
+    chosen = down == goal
+    select = chosen.astype(jnp.float32).astype(jnp.bfloat16)
+    code = jnp.sum(jnp.where(chosen, place + 1, 0), axis=1, keepdims=True).astype(jnp.float32)
+    code = jnp.broadcast_to(code, (slots, LANES)).astype(jnp.bfloat16)
+
+    piece_copies = []
     for index in range(4):
         loads[index].wait()
     for shift in range(4):
@@ -179,45 +200,26 @@
         squares = jnp.concatenate([even * even, odd * odd], axis=1)
         energy = dot_split(squares, mel_ref[0], mel_ref[1])
         logs = jnp.log(1.0 + energy).astype(jnp.bfloat16)
-        for g in groups:
-            f = 4 * g + shift
-            mel_rows[:, f * MEL : (f + 1) * MEL] = logs[g * slots : (g + 1) * slots]
-
-    loads[4].wait()
-    target = target_ref[...]
-    owner = jnp.where(target >= 0, lax.shift_right_arithmetic(target, 5), shards)
-    place = jnp.bitwise_and(target, PE - 1)
-    down = lax.broadcasted_iota(jnp.int32, (slots, slots), 0)
-    across = lax.broadcasted_iota(jnp.int32, (slots, slots), 1)
-    owner_wide = jnp.broadcast_to(owner, (slots, slots))
-    owner_down = jnp.sum(jnp.where(down == across, owner_wide, 0), axis=1, keepdims=True)
-    rank = jnp.sum(
-        jnp.where((owner_down == owner_wide) & (down < across), 1, 0), axis=0, keepdims=True
-    )
-    goal = jnp.where(owner < shards, owner * cap + rank, -1)
-    chosen = down == goal
-    select = chosen.astype(jnp.float32).astype(jnp.bfloat16)
-    rows = dot(select, mel_rows[...]).astype(jnp.bfloat16)
-    code = jnp.sum(jnp.where(chosen, place + 1, 0), axis=1, keepdims=True).astype(jnp.float32)
-    code = jnp.broadcast_to(code, (slots, LANES)).astype(jnp.bfloat16)
-    for t in range(shards):
-        packed[t, :, : FP * MEL] = rows[t * cap : (t + 1) * cap]
-        packed[t, :, FP * MEL :] = code[t * cap : (t + 1) * cap]
-
-    piece_copies = []
-    for d in range(1, shards):
-        to = lax.rem(s + d, shards)
-        copy = pltpu.make_async_remote_copy(
-            src_ref=packed.at[to],
-            dst_ref=received.at[s],
-            send_sem=asend.at[d - 1],
-            recv_sem=arecv.at[d - 1],
-            device_id={"seq": to},
-            device_id_type=MESH,
-        )
-        copy.start()
-        piece_copies.append(copy)
-    received[s] = packed[s]
+        logs = jnp.concatenate([logs[g * slots : (g + 1) * slots] for g in groups], axis=1)
+        rows = dot(select, logs).astype(jnp.bfloat16)
+        wide = len(groups) * MEL
+        for t in range(shards):
+            packed[shift][t, :, :wide] = rows[t * cap : (t + 1) * cap]
+            if shift == 0:
+                packed[0][t, :, wide:] = code[t * cap : (t + 1) * cap]
+        for d in range(1, shards):
+            to = lax.rem(s + d, shards)
+            copy = pltpu.make_async_remote_copy(
+                src_ref=packed[shift].at[to],
+                dst_ref=received[shift].at[s],
+                send_sem=asend.at[shift, d - 1],
+                recv_sem=arecv.at[shift, d - 1],
+                device_id={"seq": to},
+                device_id_type=MESH,
+            )
+            copy.start()
+            piece_copies.append(copy)
+        received[shift][s] = packed[shift][s]
 
     @pl.when(half == 0)
     def _():
@@ -247,27 +249,34 @@
         rolled = pltpu.roll(wide, TABLE - (CH - 1), 1, stride=1, stride_axis=0)
         bias_ref[row] = rolled[:, : 3 * CH]
 
-    for copy in piece_copies:
-        copy.wait_recv()
-
-    arrived = received[...]
-    if cap % 16:
-        arrived = arrived.astype(jnp.float32).reshape(slots, arrived.shape[2])
-        arrived = arrived.astype(jnp.bfloat16)
-    else:
-        arrived = arrived.reshape(slots, arrived.shape[2])
-    frame_rows = jnp.concatenate(
-        [arrived[:, f * MEL : (f + 1) * MEL] for f in range(FP)], axis=0
-    )
-    code_down = arrived[:, FP * MEL : FP * MEL + 1].astype(jnp.float32)
-    code_wide = jnp.broadcast_to(code_down, (slots, slots))
-    code_across = jnp.sum(jnp.where(down == across, code_wide, 0.0), axis=0, keepdims=True)
-    first = jnp.where(code_across > 0.5, (code_across - 1.0) * FP, -1000.0)
-    frame_at = jnp.concatenate([first + float(f) for f in range(FP)], axis=1)
+    totals = [jnp.zeros((CH, MEL), jnp.float32) for _ in range(4)]
+    for shift in range(4):
+        for d in range(1, shards):
+            piece_copies[shift * (shards - 1) + d - 1].wait_recv()
+        arrived = received[shift][...]
+        if cap % 16:
+            arrived = arrived.astype(jnp.float32).reshape(slots, arrived.shape[2])
+            arrived = arrived.astype(jnp.bfloat16)
+        else:
+            arrived = arrived.reshape(slots, arrived.shape[2])
+        groups = range((FP - shift + 3) // 4)
+        frame_rows = jnp.concatenate(
+            [arrived[:, g * MEL : (g + 1) * MEL] for g in groups], axis=0
+        )
+        if shift == 0:
+            code_down = arrived[:, len(groups) * MEL : len(groups) * MEL + 1].astype(jnp.float32)
+            code_wide = jnp.broadcast_to(code_down, (slots, slots))
+            code_across = jnp.sum(
+                jnp.where(down == across, code_wide, 0.0), axis=0, keepdims=True
+            )
+            first = jnp.where(code_across > 0.5, (code_across - 1.0) * FP, -1000.0)
+        frame_at = jnp.concatenate([first + float(4 * g + shift) for g in groups], axis=1)
+        for m in range(4):
+            token = lax.broadcasted_iota(jnp.int32, (CH, len(groups) * slots), 0) * 4 + m
+            pick = (token.astype(jnp.float32) == frame_at).astype(jnp.float32)
+            totals[m] = totals[m] + dot(pick.astype(jnp.bfloat16), frame_rows)
     for m in range(4):
-        token = lax.broadcasted_iota(jnp.int32, (CH, FP * slots), 0) * 4 + m
-        pick = (token.astype(jnp.float32) == frame_at).astype(jnp.float32).astype(jnp.bfloat16)
-        tokens_ref[h + 1, :, m * MEL : (m + 1) * MEL] = dot(pick, frame_rows).astype(jnp.bfloat16)
+        tokens_ref[h + 1, :, m * MEL : (m + 1) * MEL] = totals[m].astype(jnp.bfloat16)
 
     head_copies = []
     for d in range(1, heads):
@@ -355,7 +364,7 @@
     context_ref,
     qkv_weight, queries, keys, values, lengths_ref, sem,
 ):
-    blocks = tokens_ref.shape[0] - 2
+    blocks = tokens_ref.shape[0] // CH - 2
     heads = weights_ref.shape[0]
     width = weights_ref.shape[2]
     loads = [
@@ -368,29 +377,23 @@
     half = lax.axis_index("seq") * subs + lax.axis_index("sub")
     first_token, token_total = half * blocks * CH, shards * subs * blocks * CH
 
-    normed = []
-    for b in range(blocks + 2):
-        summed = jnp.concatenate(
-            [dot(tokens_ref[b], weights_ref[g]) + sub_bias_ref[g] for g in range(heads)], axis=1
-        )
-        value = (summed / (1.0 + jnp.exp(-summed))).astype(jnp.bfloat16).astype(jnp.float32)
-        mean = jnp.mean(value, axis=1, keepdims=True)
-        centred = value - mean
-        variance = jnp.mean(centred * centred, axis=1, keepdims=True)
-        normed.append(
-            (centred * lax.rsqrt(variance + EPSILON) * gain_ref[...]).astype(jnp.bfloat16)
-        )
+    tokens = tokens_ref[...]
+    summed = jnp.concatenate(
+        [dot(tokens, weights_ref[g]) + sub_bias_ref[g] for g in range(heads)], axis=1
+    )
+    value = (summed / (1.0 + jnp.exp(-summed))).astype(jnp.bfloat16).astype(jnp.float32)
+    mean = jnp.mean(value, axis=1, keepdims=True)
+    centred = value - mean
+    variance = jnp.mean(centred * centred, axis=1, keepdims=True)
+    normed = centred * lax.rsqrt(variance + EPSILON) * gain_ref[...]
+    normed_all = normed.astype(jnp.bfloat16)
+    normed_own = normed[CH : (blocks + 1) * CH].astype(jnp.bfloat16)
 
     for part, out in ((0, queries), (1, keys), (2, values)):
         loads[part].wait()
-        for b in range(blocks + 2):
-            if part == 0 and (b == 0 or b == blocks + 1):
-                continue
-            row = (b - 1 if part == 0 else b) * CH
-            done = dot(normed[b], qkv_weight[part]).astype(jnp.bfloat16).astype(jnp.float32)
-            if part == 0:
-                done = done * (1.0 / math.sqrt(HDIM))
-            out[row : row + CH] = done
+        rows = normed_own if part == 0 else normed_all
+        done = dot(rows, qkv_weight[part]).astype(jnp.bfloat16).astype(jnp.float32)
+        out[...] = done * (1.0 / math.sqrt(HDIM)) if part == 0 else done
 
     loads[3].wait()
     span = 3 * CH
@@ -407,27 +410,28 @@
             key_utt = key_utt + (key_pos >= end).astype(jnp.int32)
         inside = (key_pos >= 0) & (key_pos < token_total)
         key_utt = jnp.where(inside, key_utt, -1)
-        masks.append(query_utt == key_utt)
+        mask = jnp.where(query_utt == key_utt, 1.0, 0.0)
+        masks.append(jnp.concatenate([mask, mask], axis=0) > 0.5)
 
     lane = lax.broadcasted_iota(jnp.int32, (1, LANES), 1)
     for pair in range(width // LANES):
         lanes = slice(pair * LANES, (pair + 1) * LANES)
+        shift = bias_ref[2 * pair : 2 * pair + 2].reshape(2 * CH, span)
         for b in range(blocks):
             query = queries[b * CH : (b + 1) * CH, lanes]
             key = keys[b * CH : b * CH + span, lanes].astype(jnp.bfloat16)
             value = values[b * CH : b * CH + span, lanes].astype(jnp.bfloat16)
-            outs = []
-            for e in range(2):
-                mine = (lane < HDIM) if e == 0 else (lane >= HDIM)
-                own = jnp.where(mine, query, 0.0).astype(jnp.bfloat16)
-                scores = lax.dot_general(
-                    own, key, (((1,), (1,)), ((), ())), preferred_element_type=jnp.float32
-                )
-                scores = jnp.where(masks[b], scores + bias_ref[2 * pair + e], MASKED)
-                raised = jnp.exp(scores - jnp.max(scores, axis=1, keepdims=True))
-                share = 1.0 / jnp.sum(raised, axis=1, keepdims=True)
-                outs.append(dot((raised * share).astype(jnp.bfloat16), value))
-            joined = jnp.where(lane < HDIM, outs[0], outs[1]).astype(jnp.bfloat16)
+            both = jnp.concatenate(
+                [jnp.where(lane < HDIM, query, 0.0), jnp.where(lane < HDIM, 0.0, query)], axis=0
+            ).astype(jnp.bfloat16)
+            scores = lax.dot_general(
+                both, key, (((1,), (1,)), ((), ())), preferred_element_type=jnp.float32
+            )
+            scores = jnp.where(masks[b], scores + shift, MASKED)
+            raised = jnp.exp(scores - jnp.max(scores, axis=1, keepdims=True))
+            share = 1.0 / jnp.sum(raised, axis=1, keepdims=True)
+            out = dot((raised * share).astype(jnp.bfloat16), value)
+            joined = jnp.where(lane < HDIM, out[:CH], out[CH:]).astype(jnp.bfloat16)
             context_ref[b * CH : (b + 1) * CH, lanes] = joined
 
 
@@ -440,7 +444,7 @@
     depth, width = sub_weight.shape
     whole_width = qkv_weight.shape[0]
     vmem = pl.BlockSpec(memory_space=pltpu.VMEM)
-    payload = (FP + 1) * MEL
+    payloads = [((FP - shift + 3) // 4 + (shift == 0)) * MEL for shift in range(4)]
     dma = pltpu.SemaphoreType.DMA
     hbm = pl.BlockSpec(memory_space=pltpu.HBM)
     heads_here = rel_bias.shape[0]
@@ -464,12 +468,11 @@
             pltpu.VMEM((width,), jnp.bfloat16),
             pltpu.VMEM((whole_width,), jnp.float32),
             pltpu.VMEM(rel_bias.shape, jnp.float32),
-            pltpu.VMEM((slots, FP * MEL), jnp.bfloat16),
-            pltpu.VMEM((shards, cap, payload), jnp.bfloat16),
-            pltpu.VMEM((shards, cap, payload), jnp.bfloat16),
+            *[pltpu.VMEM((shards, cap, wide), jnp.bfloat16) for wide in payloads],
+            *[pltpu.VMEM((shards, cap, wide), jnp.bfloat16) for wide in payloads],
             dma((9,)),
             dma((heads - 1,)), dma((heads - 1,)), dma((heads - 1,)), dma((heads - 1,)),
-            dma((shards - 1,)), dma((shards - 1,)),
+            dma((4, shards - 1)), dma((4, shards - 1)),
             dma((heads - 1,)), dma((heads - 1,)),
             dma((2, heads)), dma((2,)), dma((heads - 1,)), dma((heads - 1,)),
         ],
@@ -511,7 +514,7 @@
         compiler_params=pltpu.CompilerParams(vmem_limit_bytes=36 << 20),
         name="back",
     )(
-        tokens,
+        tokens.reshape((heads + 2) * CH, 4 * MEL),
         weights,
         bias_rows,
         gain_row,

time: 39.4 us -> 33.1 us (0.84)
  Pallas kernels: 38.9 us -> 32.8 us
    pallas_call x1, Pallas kernels: 17.2 us -> 11.8 us  [local(): pl.pallas_call(functools.partial(back_kernel, shards, subs), out_shape=ja...]
    pallas_call x1, Pallas kernels: 21.7 us -> 21 us  [local(): pl.pallas_call(functools.partial(front_kernel, shards, heads, subs), out_...]
where the time goes in v2:
time: 33.1 us; the launch traced here: 33 us
  Pallas kernels  32.8 us (99%)
    pallas_call x1, Pallas kernels, local(): pl.pallas_call(functools.partial(front_kernel, shards, heads, subs), out_...  21 us
    pallas_call x1, Pallas kernels, local(): pl.pallas_call(functools.partial(back_kernel, shards, subs), out_shape=ja...  11.8 us

profile of v2, /device:TPU:1, one launch (start us, length us, event | category | flops | bytes accessed | tf_op | source)
XLA Modules:
  0.0 33.0 jit_solution(18383372787035852721)
XLA Ops:
  0.0 21.0 %front.1 = (bf16[4,136,512]{2,1,0:T(8,128)(2,1)S(1)}, bf16[2,512,768]{2,1,0:T(8,128)(2,1)S(1)}, f32[2,1,768]{2,1,0:T(1,128)S(1)}, f32[1,1536]{1,0:T(1,128)S(1)}, f32[12,136,408]{2,1,0:T(8,128)S(1)}) custom-call(f32[64,3072]{1,0:T(8,128)} %bitcast.6, s32[1,64]{1,0:T(1,128)} %bitcast.7, bf16[512,768]{1,0:T(8,128)(2,1)} %weight_ref.1, ...), custom_call_target="tpu_custom_call" | custom-call | tf_op jit(solution)/shard_map/front/pallas_call | solution.py:451
  21.0 11.8 %back.1 = bf16[272,768]{1,0:T(8,128)(2,1)} custom-call(bf16[544,512]{1,0:T(8,128)(2,1)S(1)} %bitcast.4, bf16[2,512,768]{2,1,0:T(8,128)(2,1)S(1)} %get-tuple-element.11.weights_ref, f32[2,1,768]{2,1,0:T(1,128)S(1)} %get-tuple-element.12.sub_bias_ref, f32[1,1536]{1,0:T(1,128)S(1)} %get-tuple-element.13.gain_ref, ...), custom_call_target="tpu_custom_call" | custom-call | tf_op jit(solution)/shard_map/back/pallas_call | solution.py:501

commit v3 on v2

--- a/solution.py
+++ b/solution.py
@@ -120,21 +120,13 @@
 
     @pl.when(half > 0)
     def _():
-        for other in range(heads):
-            pl.semaphore_signal(
-                barrier, inc=1, device_id={**place_of(half - 1), "head": other},
-                device_id_type=MESH,
-            )
+        pl.semaphore_signal(barrier, inc=1, device_id=place_of(half - 1), device_id_type=MESH)
 
     @pl.when(half < halves - 1)
     def _():
-        for other in range(heads):
-            pl.semaphore_signal(
-                barrier, inc=1, device_id={**place_of(half + 1), "head": other},
-                device_id_type=MESH,
-            )
-
-    inner = jnp.where(half > 0, heads, 0) + jnp.where(half < halves - 1, heads, 0)
+        pl.semaphore_signal(barrier, inc=1, device_id=place_of(half + 1), device_id_type=MESH)
+
+    inner = jnp.where(half > 0, 1, 0) + jnp.where(half < halves - 1, 1, 0)
     pl.semaphore_wait(barrier, shards - 1 + heads - 1 + inner)
 
     weight_copies, bias_copies = [], []
@@ -278,41 +270,47 @@
     for m in range(4):
         tokens_ref[h + 1, :, m * MEL : (m + 1) * MEL] = totals[m].astype(jnp.bfloat16)
 
+    runs = ((0, 64), (64, CH - 64))
     head_copies = []
-    for d in range(1, heads):
-        copy = pltpu.make_async_remote_copy(
-            src_ref=tokens_ref.at[h + 1],
-            dst_ref=tokens_ref.at[h + 1],
-            send_sem=hsend.at[d - 1],
-            recv_sem=hrecv.at[d - 1],
-            device_id={"head": lax.rem(h + d, heads)},
+    for run, (start, size) in enumerate(runs):
+        for d in range(1, heads):
+            copy = pltpu.make_async_remote_copy(
+                src_ref=tokens_ref.at[h + 1, pl.ds(start, size)],
+                dst_ref=tokens_ref.at[h + 1, pl.ds(start, size)],
+                send_sem=hsend.at[run, d - 1],
+                recv_sem=hrecv.at[run, d - 1],
+                device_id={"head": lax.rem(h + d, heads)},
+                device_id_type=MESH,
+            )
+            copy.start()
+            head_copies.append(copy)
+
+    def halo(to, source, row, side, run):
+        start, size = runs[run]
+        return pltpu.make_async_remote_copy(
+            src_ref=tokens_ref.at[source, pl.ds(start, size)],
+            dst_ref=tokens_ref.at[row, pl.ds(start, size)],
+            send_sem=nsend.at[side, run],
+            recv_sem=nrecv.at[side, run],
+            device_id=place_of(to),
             device_id_type=MESH,
         )
-        copy.start()
-        head_copies.append(copy)
-
-    def halo(other, to, row, side):
-        return pltpu.make_async_remote_copy(
-            src_ref=tokens_ref.at[h + 1],
-            dst_ref=tokens_ref.at[row],
-            send_sem=nsend.at[side, other],
-            recv_sem=nrecv.at[side],
-            device_id={**place_of(to), "head": other},
-            device_id_type=MESH,
-        )
-
-    sends_up = (half < halves - 1) & (h == heads - 1)
-    sends_down = (half > 0) & (h == 0)
-
-    @pl.when(sends_up)
-    def _():
-        for other in range(heads):
-            halo(other, half + 1, 0, 0).start()
-
-    @pl.when(sends_down)
-    def _():
-        for other in range(heads):
-            halo(other, half - 1, heads + 1, 1).start()
+
+    def halo_up(run):
+        return halo(half + 1, heads, 0, 0, run)
+
+    def halo_down(run):
+        return halo(half - 1, 1, heads + 1, 1, run)
+
+    def when(condition, action):
+        @pl.when(condition)
+        def _():
+            action()
+
+    has_up, has_down = half < halves - 1, half > 0
+    for run in range(2):
+        when(has_up & (h == heads - 1), lambda: halo_up(run).start())
+        when(has_down & (h == 0), lambda: halo_down(run).start())
 
     sibling = {"sub": lax.rem(u + 1, subs)}
     forward_copies = []
@@ -330,16 +328,15 @@
         copy.start()
         forward_copies.append(copy)
 
-    for copy in head_copies:
-        copy.wait_recv()
-
-    @pl.when(half > 0)
-    def _():
-        halo(0, half, 0, 0).wait_recv()
-
-    @pl.when(half < halves - 1)
-    def _():
-        halo(0, half, heads + 1, 1).wait_recv()
+    for run in range(2):
+        for d in range(1, heads):
+            head_copies[run * (heads - 1) + d - 1].wait_recv()
+        when(has_up & (h != heads - 1), lambda: halo_up(run).start())
+        when(has_down & (h != 0), lambda: halo_down(run).start())
+
+    for run in range(2):
+        when(has_down, lambda: halo_up(run).wait_recv())
+        when(has_up, lambda: halo_down(run).wait_recv())
 
     for copy in forward_copies + bias_copies:
         copy.wait_recv()
@@ -347,15 +344,9 @@
     for copy in bias_copies + weight_copies + piece_copies + head_copies + forward_copies:
         copy.wait_send()
 
-    @pl.when(sends_up)
-    def _():
-        for other in range(heads):
-            halo(other, half + 1, 0, 0).wait_send()
-
-    @pl.when(sends_down)
-    def _():
-        for other in range(heads):
-            halo(other, half - 1, heads + 1, 1).wait_send()
+    for run in range(2):
+        when(has_up, lambda: halo_up(run).wait_send())
+        when(has_down, lambda: halo_down(run).wait_send())
 
 
 def back_kernel(
@@ -473,8 +464,8 @@
             dma((9,)),
             dma((heads - 1,)), dma((heads - 1,)), dma((heads - 1,)), dma((heads - 1,)),
             dma((4, shards - 1)), dma((4, shards - 1)),
-            dma((heads - 1,)), dma((heads - 1,)),
-            dma((2, heads)), dma((2,)), dma((heads - 1,)), dma((heads - 1,)),
+            dma((2, heads - 1)), dma((2, heads - 1)),
+            dma((2, 2)), dma((2, 2)), dma((heads - 1,)), dma((heads - 1,)),
         ],
         compiler_params=pltpu.CompilerParams(
             collective_id=0, has_side_effects=True, vmem_limit_bytes=28 << 20

time: 33.1 us -> 32.5 us (0.982)
  Pallas kernels: 32.8 us -> 32.2 us
    pallas_call x1, Pallas kernels: 21 us -> 20.4 us  [local(): pl.pallas_call(functools.partial(front_kernel, shards, heads, subs), out_...]
where the time goes in v3:
time: 32.5 us; the launch traced here: 32.3 us
  Pallas kernels  32.2 us (99%)
    pallas_call x1, Pallas kernels, local(): pl.pallas_call(functools.partial(front_kernel, shards, heads, subs), out_...  20.4 us
    pallas_call x1, Pallas kernels, local(): pl.pallas_call(functools.partial(back_kernel, shards, subs), out_shape=ja...  11.8 us

profile of v3, /device:TPU:1, one launch (start us, length us, event | category | flops | bytes accessed | tf_op | source)
XLA Modules:
  0.0 32.3 jit_solution(723852145301424226)
XLA Ops:
  0.0 20.4 %front.1 = (bf16[4,136,512]{2,1,0:T(8,128)(2,1)S(1)}, bf16[2,512,768]{2,1,0:T(8,128)(2,1)S(1)}, f32[2,1,768]{2,1,0:T(1,128)S(1)}, f32[1,1536]{1,0:T(1,128)S(1)}, f32[12,136,408]{2,1,0:T(8,128)S(1)}) custom-call(f32[64,3072]{1,0:T(8,128)} %bitcast.6, s32[1,64]{1,0:T(1,128)} %bitcast.7, bf16[512,768]{1,0:T(8,128)(2,1)} %weight_ref.1, ...), custom_call_target="tpu_custom_call" | custom-call | tf_op jit(solution)/shard_map/front/pallas_call | solution.py:442
  20.4 11.8 %back.1 = bf16[272,768]{1,0:T(8,128)(2,1)} custom-call(bf16[544,512]{1,0:T(8,128)(2,1)S(1)} %bitcast.4, bf16[2,512,768]{2,1,0:T(8,128)(2,1)S(1)} %get-tuple-element.11.weights_ref, f32[2,1,768]{2,1,0:T(1,128)S(1)} %get-tuple-element.12.sub_bias_ref, f32[1,1536]{1,0:T(1,128)S(1)} %get-tuple-element.13.gain_ref, ...), custom_call_target="tpu_custom_call" | custom-call | tf_op jit(solution)/shard_map/back/pallas_call | solution.py:492
